TPU v7x, 512 devices: a whole 4x8x8 slice. The times are simulated.
512 devices in a mesh: ev: 32 (over x, y_lo, core), ch: 16 (over y_hi, z).
Axes of the slice: x: 4, y: 8 (y_hi: 2, y_lo: 4; y = y_hi * 4 + y_lo), z: 8, core: 2. Of those that a mesh axis runs over, the one named last changes fastest.
Arguments:
- spectra: float32 [512, 16, 65536], P('ev', None, 'ch'), as said below
- tile_mask: int32 [512, 512], P('ev', 'ch'), may hold values 0 or 1
- source_init: float32 [512, 16], P('ev'), may hold values from -6 to 6
- site_init: float32 [16, 65536], P(None, 'ch'), may hold values from -6 to 6
- event_pos: float32 [3, 512], P(None, 'ev'), may hold values from 5 to 50
- channel_pos: float32 [2, 65536], P(None, 'ch'), may hold values from 0 to 50
- atten: float32 [16], replicated, may hold values from 0.02 to 0.3
Outputs:
- source: float32 [512, 16], P('ev')
- site: float32 [16, 65536], P(None, 'ch')
Inputs may be any that keep to these rules, and one draw needn't show every extreme that they name: spectra are log amplitudes of order one to a few, with outliers. `tile_mask`: 0 marks an event invalid on a whole tile of 128 channels.
All inputs are finite; a program needn't handle non-finite values. No bound on the sum of `tile_mask` on one device may be relied on, other than what follows from the above.
Results may differ from a plain program's by a relative error of at most 0.0001.
Values sent between devices are 32-bit elements; how exact they have to be, the bound alone decides.
A program may use at most 64 MiB of HBM per device.

v0:
```python
import jax
import jax.numpy as jnp
from jax import lax
from jax.sharding import PartitionSpec as P

ITERS = 2


def on_device(spectra, tile_mask, source_init, site_init, event_pos, channel_pos, atten):
    ev_n, freqs, ch_n = spectra.shape
    total_ch = ch_n * lax.axis_size("ch")
    valid = jnp.repeat(tile_mask, 128, axis=1).astype(jnp.float32)[:, None, :]
    count_part = jnp.sum(valid)
    east = event_pos[0][:, None] - channel_pos[0][None, :]
    north = event_pos[1][:, None] - channel_pos[1][None, :]
    depth = event_pos[2][:, None]
    travel = jnp.sqrt(east * east + north * north + depth * depth) / 3.0
    path = atten[None, :, None] * travel[:, None, :]
    source = source_init
    site = site_init
    for step in range(ITERS):
        resid = spectra - source[:, :, None] - site[None, :, :] + path
        abs_part = jnp.sum(valid * jnp.abs(resid), axis=(0, 2))
        absum, count = lax.psum((abs_part, count_part), ("ev", "ch"))
        delta = 1.345 * (1.2533 * absum / jnp.maximum(count, 1.0) + 1e-05)
        limit = delta[None, :, None]
        weight = limit / jnp.maximum(jnp.abs(resid), limit) * valid
        product = weight * resid
        src_num, src_den = lax.psum((jnp.sum(product, axis=2), jnp.sum(weight, axis=2)), "ch")
        site_num = jnp.sum(product, axis=0)
        site_den = jnp.sum(weight, axis=0)
        site_num, site_den = lax.psum((site_num, site_den), "ev")
        site = site + 0.5 * site_num / (site_den + 1.0)
        source = source + 0.5 * src_num / (src_den + 1.0)
        shift = lax.psum(jnp.sum(site, axis=1), "ch") / total_ch
        site = site - shift[:, None]
        source = source + shift[None, :]
    return (source, site)


def solution(mesh):
    in_specs = (
        P("ev", None, "ch"),
        P("ev", "ch"),
        P("ev", None),
        P(None, "ch"),
        P(None, "ev"),
        P(None, "ch"),
        P(),
    )
    out_specs = (P("ev", None), P(None, "ch"))
    return jax.shard_map(
        on_device, mesh=mesh, in_specs=in_specs, out_specs=out_specs, check_vma=False
    )
```

profile of v0, /device:TPU:8, one launch (start us, length us, event | category | flops | bytes accessed | tf_op | source)
XLA Modules:
  0.0 981.2 jit_solution(700504949465934503)
XLA Ops:
  7.2 0.0 copy-start.2
  7.2 0.0 copy-start
  7.2 0.0 copy-start.1
  7.2 0.0 all-reduce.10.cloned.1.call-start
  7.2 0.8 slice_bitcast_fusion.1
  8.0 0.7 convert_element_type.13
  8.7 0.9 fusion.8
  9.6 0.1 broadcast_in_dim.2
  9.7 0.2 copy.11
  9.9 0.2 sqrt_multiply_fusion
  10.1 3.4 multiply_reduce_fusion.1
  13.5 0.7 broadcast_reduce_fusion
  14.2 104.9 %all-reduce = (f32[16]{0:T(128)S(1)}, f32[]{:T(128)}) all-reduce(f32[16]{0:T(128)S(1)} %multiply_reduce_fusion.1, f32[]{:T(128)} %broadcast_reduce_fusion), channel_id=1, replica_groups=mesh['ev'=32,'ch'=16] {'ev','ch'}, use_global_device_ids=true, to_apply=%region_1.0 | all-reduce | flops 17 | bytes 136 | tf_op jit(solution)/shard_map/psum | solution.py:24
  119.7 0.0 copy-done.2
  119.8 0.0 copy-done
  119.8 0.0 copy-done.1
  119.8 5.4 fusion.4
  125.1 0.0 all-reduce.10.cloned.1.call-update
  125.2 0.0 all-reduce.8.cloned.1.call-start
  125.2 271.7 %all-reduce.10.cloned.1.call-done = (f32[16,4096]{1,0:T(8,128)}, f32[16,4096]{1,0:T(8,128)}) async-done(((f32[16,4096]{1,0:T(8,128)}, f32[16,4096]{1,0:T(8,128)}), (f32[16,4096]{1,0:T(8,128)}, f32[16,4096]{1,0:T(8,128)})) %all-reduce.10.cloned.1.call-update) | async-done | bytes 524304 | tf_op jit(solution)/shard_map/psum | solution.py:32
  397.0 1.2 fusion.7
  398.2 98.8 %all-reduce.4 = (f32[16,16]{1,0:T(8,128)S(1)}, f32[16,16]{1,0:T(8,128)S(1)}, f32[16]{0:T(128)S(1)}) all-reduce(f32[16,16]{1,0:T(8,128)S(1)} %get-tuple-element.9, f32[16,16]{1,0:T(8,128)S(1)} %get-tuple-element.5, f32[16]{0:T(128)S(1)} %get-tuple-element.24), channel_id=1, replica_groups=mesh['ev'=32,'ch'=16] {'ch'}, use_global_device_ids=true, to_apply=%region_7.0 | all-reduce | flops 528 | bytes 4224 | tf_op jit(solution)/shard_map/psum | solution.py:29
  497.0 0.1 broadcast_subtract_fusion.1
  497.1 3.3 multiply_reduce_fusion
  500.4 97.2 %psum.101 = f32[16]{0:T(128)S(1)} all-reduce(f32[16]{0:T(128)S(1)} %multiply_reduce_fusion), channel_id=1, replica_groups=mesh['ev'=32,'ch'=16] {'ev','ch'}, use_global_device_ids=true, to_apply=%region_15.0 | all-reduce | flops 16 | bytes 128 | tf_op jit(solution)/shard_map/psum | solution.py:24
  597.6 5.4 fusion.2
  602.9 0.0 all-reduce.8.cloned.1.call-update
  603.0 270.0 %all-reduce.8.cloned.1.call-done = (f32[16,4096]{1,0:T(8,128)}, f32[16,4096]{1,0:T(8,128)}) async-done(((f32[16,4096]{1,0:T(8,128)}, f32[16,4096]{1,0:T(8,128)}), (f32[16,4096]{1,0:T(8,128)}, f32[16,4096]{1,0:T(8,128)})) %all-reduce.8.cloned.1.call-update) | async-done | bytes 524304 | tf_op jit(solution)/shard_map/psum | solution.py:32
  872.9 1.2 fusion.6
  874.2 98.8 %all-reduce.3 = (f32[16,16]{1,0:T(8,128)S(1)}, f32[16,16]{1,0:T(8,128)S(1)}, f32[16]{0:T(128)S(1)}) all-reduce(f32[16,16]{1,0:T(8,128)S(1)} %get-tuple-element.7, f32[16,16]{1,0:T(8,128)S(1)} %get-tuple-element.3, f32[16]{0:T(128)S(1)} %get-tuple-element.22), channel_id=1, replica_groups=mesh['ev'=32,'ch'=16] {'ch'}, use_global_device_ids=true, to_apply=%region_19.0 | all-reduce | flops 528 | bytes 4224 | tf_op jit(solution)/shard_map/psum | solution.py:29
  973.0 0.8 broadcast_subtract_fusion
  973.8 0.6 add_add_fusion
  (5 shorter events, 0.0 us)
Async XLA Ops:
  7.2 112.6 %copy-start.2 = (f32[16]{0:T(128)S(1)}, f32[16]{0:T(128)}, u32[]{:S(2)}) copy-start(f32[16]{0:T(128)} %param.13) | copy-start | bytes 196
  7.2 112.6 %copy-start = (f32[16,4096]{1,0:T(8,128)S(1)}, f32[16,4096]{1,0:T(8,128)}, u32[]{:S(2)}) copy-start(f32[16,4096]{1,0:T(8,128)} %param.10) | copy-start | bytes 786436
  7.2 112.6 %copy-start.1 = (f32[16,16]{1,0:T(8,128)S(1)}, f32[16,16]{1,0:T(8,128)}, u32[]{:S(2)}) copy-start(f32[16,16]{1,0:T(8,128)} %param.9) | copy-start | bytes 3076
  7.2 389.8 %all-reduce.10.cloned.1.call-start = ((), (), s32[]{:S(2)}) async-start(), calls=%async_computation.1 | async-start | bytes 1048576 | tf_op jit(solution)/shard_map/psum | solution.py:32
  125.2 747.8 %all-reduce.8.cloned.1.call-start = ((), (), s32[]{:S(2)}) async-start(), calls=%async_computation | async-start | bytes 1048576 | tf_op jit(solution)/shard_map/psum | solution.py:32
Sparse Core Ops, SparseCore 0:
  125.3 271.6 all-reduce.9
  603.1 269.8 all-reduce.7
where the time goes:
time: 982 us; the launch traced here: 981 us
  waiting for transfers between devices  542 us (55%)
  blocking collectives  400 us (41%)
  other arithmetic  23.8 us (2%)
  between operations  14.8 us (2%)
    psum x2, waiting for transfers between devices, on_device(): site_num, site_den = lax.psum((site_num, site_den), 'ev')  542 us
    psum x2, blocking collectives, on_device(): absum, count = lax.psum((abs_part, count_part), ('ev', 'ch'))  202 us
    psum x2, blocking collectives, on_device(): lax.psum((jnp.sum(product, axis=2), jnp.sum(weight, axis=2)), 'ch')  198 us
  transfers between devices with their start and end apart: 2, of which 2 were waited for; matrix products, arithmetic and copies ran while one was open for 0% of the time, Pallas kernels for 0%

commit v1 on v0

--- a/solution.py
+++ b/solution.py
@@ -21,7 +21,7 @@
     for step in range(ITERS):
         resid = spectra - source[:, :, None] - site[None, :, :] + path
         abs_part = jnp.sum(valid * jnp.abs(resid), axis=(0, 2))
-        absum, count = lax.psum((abs_part, count_part), ("ev", "ch"))
+        absum, count = lax.psum(lax.psum((abs_part, count_part), "ch"), "ev")
         delta = 1.345 * (1.2533 * absum / jnp.maximum(count, 1.0) + 1e-05)
         limit = delta[None, :, None]
         weight = limit / jnp.maximum(jnp.abs(resid), limit) * valid

time: 982 us -> 1020 us (1.039)
  blocking collectives: 400 us -> 434 us
    psum x2 -> x4, blocking collectives: 202 us -> 236 us  [on_device(): absum, count = lax.psum(lax.psum((abs_part, count_part), 'ch'), 'ev')]
where the time goes in v1:
time: 1020 us
  waiting for transfers between devices  544 us (53%)
  blocking collectives  434 us (43%)
  other arithmetic  23.8 us (2%)
  between operations  14.8 us (1%)
    psum x2, waiting for transfers between devices, on_device(): site_num, site_den = lax.psum((site_num, site_den), 'ev')  544 us
    psum x4, blocking collectives, on_device(): absum, count = lax.psum(lax.psum((abs_part, count_part), 'ch'), 'ev')  236 us
    psum x2, blocking collectives, on_device(): lax.psum((jnp.sum(product, axis=2), jnp.sum(weight, axis=2)), 'ch')  198 us
  transfers between devices with their start and end apart: 2, of which 2 were waited for; matrix products, arithmetic and copies ran while one was open for 0% of the time, Pallas kernels for 0%

profile of v1, /device:TPU:8, one launch (start us, length us, event | category | flops | bytes accessed | tf_op | source)
XLA Modules:
  0.0 1017.7 jit_solution(4027297676388822308)
XLA Ops:
  7.2 0.0 copy-start.2
  7.2 0.0 copy-start
  7.2 0.0 copy-start.1
  7.2 0.0 all-reduce.11.cloned.1.call-start
  7.2 0.8 slice_bitcast_fusion.1
  8.0 0.7 convert_element_type.13
  8.7 0.7 broadcast_reduce_fusion
  9.5 0.9 fusion.8
  10.3 0.1 broadcast_in_dim.2
  10.5 0.2 copy.11
  10.6 0.2 sqrt_multiply_fusion
  10.8 3.4 multiply_reduce_fusion.1
  14.2 60.3 %all-reduce.5 = (f32[16]{0:T(128)S(1)}, f32[]{:T(128)}) all-reduce(f32[16]{0:T(128)S(1)} %multiply_reduce_fusion.1, f32[]{:T(128)} %broadcast_reduce_fusion), channel_id=1, replica_groups=mesh['ev'=32,'ch'=16] {'ch'}, use_global_device_ids=true, to_apply=%region_1.0 | all-reduce | flops 17 | bytes 136 | tf_op jit(solution)/shard_map/psum | solution.py:24
  74.5 63.2 %all-reduce = (f32[16]{0:T(128)S(1)}, f32[]{:T(128)}) all-reduce(f32[16]{0:T(128)S(1)} %get-tuple-element.22, f32[]{:T(128)} %get-tuple-element.23), channel_id=1, replica_groups=mesh['ev'=32,'ch'=16] {'ev'}, use_global_device_ids=true, to_apply=%region_2.0 | all-reduce | flops 17 | bytes 136 | tf_op jit(solution)/shard_map/psum | solution.py:24
  138.3 0.0 copy-done.2
  138.3 5.4 fusion.4
  143.7 0.0 all-reduce.11.cloned.1.call-update
  143.7 0.0 all-reduce.9.cloned.1.call-start
  143.8 271.0 %all-reduce.11.cloned.1.call-done = (f32[16,4096]{1,0:T(8,128)}, f32[16,4096]{1,0:T(8,128)}) async-done(((f32[16,4096]{1,0:T(8,128)}, f32[16,4096]{1,0:T(8,128)}), (f32[16,4096]{1,0:T(8,128)}, f32[16,4096]{1,0:T(8,128)})) %all-reduce.11.cloned.1.call-update) | async-done | bytes 524304 | tf_op jit(solution)/shard_map/psum | solution.py:32
  414.8 1.2 fusion.7
  416.0 98.8 %all-reduce.4 = (f32[16,16]{1,0:T(8,128)S(1)}, f32[16,16]{1,0:T(8,128)S(1)}, f32[16]{0:T(128)S(1)}) all-reduce(f32[16,16]{1,0:T(8,128)S(1)} %get-tuple-element.9, f32[16,16]{1,0:T(8,128)S(1)} %get-tuple-element.5, f32[16]{0:T(128)S(1)} %get-tuple-element.26), channel_id=1, replica_groups=mesh['ev'=32,'ch'=16] {'ch'}, use_global_device_ids=true, to_apply=%region_9.0 | all-reduce | flops 528 | bytes 4224 | tf_op jit(solution)/shard_map/psum | solution.py:29
  514.8 0.1 broadcast_subtract_fusion.1
  514.9 3.3 multiply_reduce_fusion
  518.2 46.2 %psum.127 = f32[16]{0:T(128)S(1)} all-reduce(f32[16]{0:T(128)S(1)} %multiply_reduce_fusion), channel_id=1, replica_groups=mesh['ev'=32,'ch'=16] {'ch'}, use_global_device_ids=true, to_apply=%region_17.0 | all-reduce | flops 16 | bytes 128 | tf_op jit(solution)/shard_map/psum | solution.py:24
  564.5 66.6 %psum.128 = f32[16]{0:T(128)S(1)} all-reduce(f32[16]{0:T(128)S(1)} %psum.127), channel_id=1, replica_groups=mesh['ev'=32,'ch'=16] {'ev'}, use_global_device_ids=true, to_apply=%region_18.0 | all-reduce | flops 16 | bytes 128 | tf_op jit(solution)/shard_map/psum | solution.py:24
  631.1 5.4 fusion.2
  636.4 0.0 all-reduce.9.cloned.1.call-update
  636.5 273.0 %all-reduce.9.cloned.1.call-done = (f32[16,4096]{1,0:T(8,128)}, f32[16,4096]{1,0:T(8,128)}) async-done(((f32[16,4096]{1,0:T(8,128)}, f32[16,4096]{1,0:T(8,128)}), (f32[16,4096]{1,0:T(8,128)}, f32[16,4096]{1,0:T(8,128)})) %all-reduce.9.cloned.1.call-update) | async-done | bytes 524304 | tf_op jit(solution)/shard_map/psum | solution.py:32
  909.4 1.2 fusion.6
  910.7 98.8 %all-reduce.3 = (f32[16,16]{1,0:T(8,128)S(1)}, f32[16,16]{1,0:T(8,128)S(1)}, f32[16]{0:T(128)S(1)}) all-reduce(f32[16,16]{1,0:T(8,128)S(1)} %get-tuple-element.7, f32[16,16]{1,0:T(8,128)S(1)} %get-tuple-element.3, f32[16]{0:T(128)S(1)} %get-tuple-element.24), channel_id=1, replica_groups=mesh['ev'=32,'ch'=16] {'ch'}, use_global_device_ids=true, to_apply=%region_22.0 | all-reduce | flops 528 | bytes 4224 | tf_op jit(solution)/shard_map/psum | solution.py:29
  1009.5 0.8 broadcast_subtract_fusion
  1010.3 0.6 add_add_fusion
  (7 shorter events, 0.0 us)
Async XLA Ops:
  7.2 131.1 %copy-start.2 = (f32[16]{0:T(128)S(1)}, f32[16]{0:T(128)}, u32[]{:S(2)}) copy-start(f32[16]{0:T(128)} %param.13) | copy-start | bytes 196
  7.2 131.1 %copy-start = (f32[16,4096]{1,0:T(8,128)S(1)}, f32[16,4096]{1,0:T(8,128)}, u32[]{:S(2)}) copy-start(f32[16,4096]{1,0:T(8,128)} %param.10) | copy-start | bytes 786436
  7.2 131.1 %copy-start.1 = (f32[16,16]{1,0:T(8,128)S(1)}, f32[16,16]{1,0:T(8,128)}, u32[]{:S(2)}) copy-start(f32[16,16]{1,0:T(8,128)} %param.9) | copy-start | bytes 3076
  7.2 407.6 %all-reduce.11.cloned.1.call-start = ((), (), s32[]{:S(2)}) async-start(), calls=%async_computation.1 | async-start | bytes 1048576 | tf_op jit(solution)/shard_map/psum | solution.py:32
  143.7 765.7 %all-reduce.9.cloned.1.call-start = ((), (), s32[]{:S(2)}) async-start(), calls=%async_computation | async-start | bytes 1048576 | tf_op jit(solution)/shard_map/psum | solution.py:32
Sparse Core Ops, SparseCore 0:
  143.8 270.8 all-reduce.10
  636.6 272.8 all-reduce.8
